TPU v7x, 32 devices: a whole 2x2x4 slice. The times are simulated.
32 devices in a mesh: gx: 8 (over z, y), gy: 4 (over x, core).
Axes of the slice: x: 2, y: 2, z: 4, core: 2. Of those that a mesh axis runs over, the one named last changes fastest.
Arguments:
- positions: float32 [3, 8192, 128], P(None, ('gx', 'gy')), may hold values from 0 to 1
- masses: float32 [8192, 128], P(('gx', 'gy')), may hold values from 0.004 to 0.012
- smoothing: float32 [8192, 128], P(('gx', 'gy')), may hold values from 0.55 to 1
- entropy: float32 [8192, 128], P(('gx', 'gy')), may hold values from 0.5 to 2
- density: float32 [8192, 128], P(('gx', 'gy')), may hold values from 0.5 to 2
- active_cells: int32 [128], P(('gx', 'gy')), may hold values from 0 to 8191, as said below
- active_count: int32 [32], P(('gx', 'gy')), may hold values from 1 to 4, 84 in all
- neighbours: int32 [128, 27], P(('gx', 'gy')), may hold values from 0 to 8191, as said below
- mig_source: int32 [4096], P(('gx', 'gy')), may hold values from 0 to 32767
- mig_dest: int32 [4096, 1], P(('gx', 'gy')), may hold values from 0 to 31; in each aligned block of 128 rows (0 to 127, 128 to 255, ...) at most 8 rows name the same one
Outputs:
- new_density: float32 [8192, 128], P(('gx', 'gy'))
- acceleration: float32 [3, 128, 128], P(None, ('gx', 'gy'))
- arrivals: float32 [7, 8192], P(None, ('gx', 'gy'))
Inputs may be any that keep to these rules, and one draw needn't show every extreme that they name: `active_cells`: the 4 entries of device d are distinct cells of device d. The middle entry (index 13) of a slot is its active cell. Every other entry is a cell of the slot's own device, or a cell of the device just before or just after it in the cell order lying within 64 cells of the end they share. Over all slots of one device, at most 8 distinct cells of each of these two devices are named, and every device with neighbours on both sides names exactly 8 on each side. `mig_dest`: within the 128 rows of one device no destination appears more than 8 times; some destination appears exactly 8 times.
All inputs are finite; a program needn't handle non-finite values. No bound on the sum of `active_count` on one device may be relied on, other than what follows from the above.
Results may differ from a plain program's by a relative error of at most 0.0003.
Values sent between devices are 32-bit elements; how exact they have to be, the bound alone decides.
No kernel may reach another device: no remote copies, remote signals or barrier semaphores. Data moves between devices by JAX's collectives and lax.ppermute only.
A program may use at most 64 MiB of HBM per device.

v0:
```python
import functools
import math

import jax
import jax.numpy as jnp
from jax import lax
from jax.experimental import pallas as pl
from jax.experimental.pallas import tpu as pltpu
from jax.sharding import PartitionSpec as P

P_SIZE = 128
NBR = 27
RIM = 64
STATE = 7
PLANES = 6
SUM_GROUP = 8
EARLY_FIRST = 6
EARLY = 13
JOBS = 10
ITEMS = 4
TINY = 1e-9
AXES = ("gx", "gy")

kernel_norm = 8.0 / math.pi
log_six_norm = math.log(6.0 * kernel_norm)
f32 = jnp.float32
bf16 = jnp.bfloat16
VMEM = pl.BlockSpec(memory_space=pltpu.VMEM)
SMEM = pl.BlockSpec(memory_space=pltpu.SMEM)
HBM = pl.BlockSpec(memory_space=pltpu.HBM)
PARAMS = pltpu.CompilerParams(vmem_limit_bytes=16 << 20)


def in_hbm(value):
    return pltpu.with_memory_space_constraint(value, pltpu.HBM)


def own_index():
    return lax.axis_index("gx") * lax.axis_size("gy") + lax.axis_index("gy")


def beta_of(inverse_len, entropy, density):
    power = 0.5 * (log_six_norm + jnp.log(entropy)) - jnp.log(density) * (1.0 / 6.0)
    return inverse_len * inverse_len * jnp.exp(power)


def row_sums(block):
    return jnp.sum(block.T, axis=0, keepdims=True)


def offset_tile(entry):
    row = lax.broadcasted_iota(jnp.int32, (8, P_SIZE), 0)
    shift = (entry // 9 - 1, entry // 3 % 3 - 1, entry % 3 - 1)
    tile = jnp.zeros((8, P_SIZE), f32)
    for axis in range(3):
        if shift[axis]:
            tile = jnp.where(row == axis, float(shift[axis]), tile)
    return tile


def split(value):
    high = value.astype(bf16).astype(f32)
    rest = value - high
    middle = rest.astype(bf16).astype(f32)
    return high, middle, rest - middle


def start_copies(pairs, sems):
    copies = [pltpu.make_async_copy(src, dst, sems.at[i]) for i, (src, dst) in enumerate(pairs)]
    for copy in copies:
        copy.start()
    return copies


def put(tab_ref, cell, count, row, plane):
    tab_ref[pl.ds(cell * 8 + row, count, stride=8), :] = plane


def tile_of(tab_ref, cell):
    return tab_ref[pl.ds(pl.multiple_of(cell * 8, 8), 8), :]


def put_table(tab_ref, cell, count, x, y, z, mass, inverse_len, beta):
    cube_root = jnp.exp(jnp.log(mass) * (1.0 / 3.0))
    planes = (x - 0.5, y - 0.5, z - 0.5, None, cube_root, mass, inverse_len, beta)
    for row, plane in enumerate(planes):
        if plane is not None:
            put(tab_ref, cell, count, row, plane)


def pack_kernel(
    pos_hbm,
    mass_hbm,
    len_hbm,
    ent_hbm,
    rho_hbm,
    act_hbm,
    nbr_hbm,
    cnt_ref,
    b_ref,
    a_ref,
    act_ref,
    nbr_ref,
    rim_ref,
    sems,
):
    cells = mass_hbm.shape[0]
    me = own_index()
    odd = me % 2
    start_a = pl.multiple_of((1 - odd) * (cells - RIM), RIM)
    start_b = pl.multiple_of(odd * (cells - RIM), RIM)
    sides = ((b_ref, start_b), (a_ref, start_a))
    pairs = [(act_hbm, act_ref)]
    for side, (out_ref, start) in enumerate(sides):
        rows = pl.ds(start, RIM)
        for index, ref in enumerate((len_hbm, ent_hbm, rho_hbm)):
            pairs.append((ref.at[rows, :], rim_ref.at[side, index]))
    first = len(pairs)
    for out_ref, start in sides:
        rows = pl.ds(start, RIM)
        for axis in range(3):
            pairs.append((pos_hbm.at[axis, rows, :], out_ref.at[pl.ds(axis * RIM, RIM), :]))
        pairs.append((mass_hbm.at[rows, :], out_ref.at[pl.ds(3 * RIM, RIM), :]))
    pairs.append((nbr_hbm, nbr_ref))
    copies = start_copies(pairs, sems)
    for copy in copies[:first]:
        copy.wait()
    lane = lax.broadcasted_iota(jnp.int32, (8, P_SIZE), 1)
    names = jnp.full((8, P_SIZE), -1.0, f32)
    slots = act_ref.shape[0]
    for slot in range(slots):
        mine = act_ref[slot] - me * cells
        live = slot < cnt_ref[0]
        names = jnp.where(jnp.logical_and(lane == slot, live), mine.astype(f32), names)
    cell = lax.broadcasted_iota(jnp.int32, (RIM, P_SIZE), 0)
    for side, (out_ref, start) in enumerate(sides):
        inverse_len = 1.0 / rim_ref[side, 0]
        beta = beta_of(inverse_len, rim_ref[side, 1], rim_ref[side, 2])
        for slot in range(slots):
            mine = jnp.where(slot < cnt_ref[0], act_ref[slot] - me * cells - start, -1)
            beta = jnp.where(cell == mine, 0.0, beta)
        out_ref[pl.ds(4 * RIM, RIM), :] = inverse_len
        out_ref[pl.ds(5 * RIM, RIM), :] = beta
        out_ref[pl.ds(PLANES * RIM, 8), :] = names
    for copy in copies[first:]:
        copy.wait()


def squared_length(tile):
    square = tile * tile
    return square[0:1, :] + square[1:2, :] + square[2:3, :]


def row_ids():
    return lax.broadcasted_iota(jnp.int32, (8, P_SIZE), 0)


def own_features(tile, scale):
    row = row_ids()
    lead = jnp.where(row < 3, -2.0 * tile, 1.0)
    lead = jnp.where(row == 4, squared_length(tile), lead)
    lead = jnp.where(row < 5, lead * scale, 0.0)
    high, middle, low = split(lead)
    return jnp.concatenate([high, high, middle, middle, high, low], axis=0).T.astype(bf16)


def other_features(tile):
    high, middle, low = split(tile)
    return jnp.concatenate([high, middle, high, middle, low, high], axis=0).astype(bf16)


def groups(size):
    return [range(first, min(first + size, NBR)) for first in range(0, NBR, size)]


def early(slot):
    return EARLY if slot else EARLY_FIRST


def stencil_tile(tab_ref, off_ref, cell, offset):
    tile = tile_of(tab_ref, cell) + tile_of(off_ref, offset)
    return jnp.where(row_ids() == 3, squared_length(tile), tile)


def density_terms(left, tiles, weights):
    row = row_ids()
    parts, roots, kept = [], [], []
    for tile, weight in zip(tiles, weights):
        root = tile[4:5, :] if weight is None else tile[4:5, :] * weight
        one = jnp.where(row == 4, 1.0, tile)
        parts.append(other_features(one * (root * root)))
        roots.append(root)
        kept.append(one)
    squares = jnp.dot(left, jnp.concatenate(parts, axis=1), preferred_element_type=f32)
    outer_sum = inner_sum = None
    for place, root in enumerate(roots):
        square = squares[:, place * P_SIZE : (place + 1) * P_SIZE]
        square = jnp.maximum(square, kept[place][6:7, :] * TINY)
        ratio = square * lax.rsqrt(square)
        outer = jnp.maximum(root - ratio, 0.0)
        inner = jnp.maximum(0.5 * root - ratio, 0.0)
        outer, inner = outer * outer * outer, inner * inner * inner
        outer_sum = outer if outer_sum is None else outer_sum + outer
        inner_sum = inner if inner_sum is None else inner_sum + inner
    return outer_sum, inner_sum, kept


def place_of(slot, position):
    return slot * NBR + position


def migrant_kernel(
    capacity,
    pos_hbm,
    mass_hbm,
    len_hbm,
    ent_hbm,
    rho_hbm,
    source_hbm,
    dest_hbm,
    act_ref,
    cnt_ref,
    nbr_ref,
    ent_ref,
    rho_ref,
    dest_ref,
    tab_ref,
    base_ref,
    code_ref,
    place_ref,
    pick_ref,
    near_ref,
    left_ref,
    total_ref,
    off_ref,
    cell_ref,
    offset_ref,
    job_ref,
    span_ref,
    pos_ref,
    mass_ref,
    len_ref,
    source_ref,
    sems,
):
    cells = mass_hbm.shape[0]
    me = own_index()
    targets = base_ref.shape[0]
    slots = act_ref.shape[0]
    base = me * cells - RIM
    copies = start_copies(
        (
            (len_hbm, len_ref),
            (ent_hbm, ent_ref),
            (rho_hbm, rho_ref),
            (pos_hbm, pos_ref),
            (mass_hbm, mass_ref),
            (source_hbm, source_ref),
            (dest_hbm, dest_ref),
        ),
        sems,
    )
    for entry in range(NBR):
        off_ref[pl.ds(entry * 8, 8), :] = offset_tile(entry)
    owned = []
    for slot in range(slots):
        mine = jnp.int32(0)
        for entry in range(NBR):
            cell = nbr_ref[slot, entry] - base
            near_by = jnp.logical_and(cell >= RIM, cell < RIM + cells)
            at = jnp.where(near_by, mine, NBR - 1 - entry + mine)
            cell_ref[place_of(slot, at)] = cell
            offset_ref[place_of(slot, at)] = entry
            mine = mine + jnp.where(near_by, 1, 0)
        owned.append(mine)
    at = jnp.int32(0)
    for slot in range(slots):
        for position in range(early(slot)):
            job_ref[at + 1] = place_of(slot, position)
            span_ref[at] = slot * P_SIZE
            at = at + jnp.where(position >= owned[slot], 1, 0)
    job_ref[0] = at
    width = targets * capacity
    column = lax.broadcasted_iota(jnp.int32, (P_SIZE, width), 1)
    spot_of = lax.broadcasted_iota(jnp.int32, (P_SIZE, width), 0) - column % capacity
    for index in range(STATE):
        hit = jnp.where(spot_of == index * capacity, 1.0, 0.0)
        pick_ref[:, pl.ds(index * width, width)] = hit.astype(bf16)
    for copy in copies:
        copy.wait()
    inverse_len = 1.0 / len_ref[...]
    beta = beta_of(inverse_len, ent_ref[...], rho_ref[...])
    put_table(
        tab_ref, RIM, cells, pos_ref[0], pos_ref[1], pos_ref[2], mass_ref[...], inverse_len, beta
    )
    for slot in range(slots):
        home = act_ref[slot] - base
        own = tile_of(tab_ref, home)
        inverse_len = own[6:7, :]
        left = own_features(own, inverse_len * inverse_len)
        left_ref[pl.ds(slot * P_SIZE, P_SIZE), :] = left
        outer_sum = jnp.zeros((P_SIZE, P_SIZE), f32)
        inner_sum = jnp.zeros((P_SIZE, P_SIZE), f32)
        for first in range(0, early(slot), 2):
            tiles, weights = [], []
            positions = range(first, min(first + 2, early(slot)))
            for position in positions:
                valid = position < owned[slot]
                cell = jnp.where(valid, cell_ref[place_of(slot, position)], home)
                offset = jnp.where(valid, offset_ref[place_of(slot, position)], 0)
                tiles.append(stencil_tile(tab_ref, off_ref, cell, offset))
                weights.append(jnp.where(valid, 1.0, 0.0))
            outer, inner, kept = density_terms(left, tiles, weights)
            outer_sum, inner_sum = outer_sum + outer, inner_sum + inner
            for position, tile in zip(positions, kept):
                near_ref[pl.ds(place_of(slot, position) * 8, 8), :] = tile
        total_ref[pl.ds(slot * P_SIZE, P_SIZE), :] = outer_sum - 4.0 * inner_sum
    source = source_ref[...]
    cell_row = source // P_SIZE
    code_row = jnp.zeros_like(source)
    for slot in range(act_ref.shape[0]):
        mine = act_ref[slot] - me * cells
        named = jnp.logical_and(cell_row == mine, slot < cnt_ref[0])
        code_row = jnp.where(named, slot + 1, code_row)
    row_id = lax.broadcasted_iota(jnp.int32, (8, P_SIZE), 0)
    stack = jnp.zeros((8, P_SIZE), f32)
    for index, part in enumerate((cell_row, source % P_SIZE, dest_ref[...], code_row)):
        stack = jnp.where(row_id == index, part.astype(f32), stack)
    columns = stack.T
    shape = (P_SIZE, P_SIZE)
    cell, lane_of, dest, code = [jnp.broadcast_to(columns[:, i : i + 1], shape) for i in range(4)]
    lane = lax.broadcasted_iota(jnp.int32, shape, 1)
    row = lax.broadcasted_iota(jnp.int32, shape, 0)
    lane_f = lane.astype(f32)
    hit = lane_f == lane_of
    same = jnp.logical_and(dest == dest_ref[...].astype(f32), lane < row)
    rank = jnp.sum(jnp.where(same, 1.0, 0.0), axis=1, keepdims=True)
    wide = lax.broadcasted_iota(jnp.int32, (P_SIZE, cells), 1).astype(f32)
    pick = jnp.where(wide == columns[:, 0:1], 1.0, 0.0).astype(bf16)
    spot = lane_f - rank
    sent = jnp.zeros(shape, f32)
    planes = [pos_ref[0], pos_ref[1], pos_ref[2], mass_ref[...], len_ref[...], ent_ref[...], rho_ref[...]]
    for index, plane in enumerate(planes):
        found = sum(
            jnp.dot(pick, piece.astype(bf16), preferred_element_type=f32) for piece in split(plane)
        )
        keep = jnp.logical_and(hit, code == 0.0) if index == STATE - 1 else hit
        value = jnp.sum(jnp.where(keep, found, 0.0), axis=1, keepdims=True)
        sent = jnp.where(spot == float(index * capacity), value, sent)
    aim = lax.broadcasted_iota(jnp.int32, (targets, P_SIZE), 0) == dest_ref[...]
    aim = jnp.where(aim, 1.0, 0.0)
    base_ref[...] = jnp.dot(aim, sent, precision=lax.Precision.HIGHEST, preferred_element_type=f32)
    code_ref[...] = jnp.where(hit, code, 0.0)
    place_ref[...] = jnp.where(spot == float((STATE - 1) * capacity), 1.0, 0.0)


def density_kernel(
    rho_in,
    ent_ref,
    a_ref,
    b_ref,
    tab_in,
    near_in,
    base_ref,
    code_ref,
    place_ref,
    dest_ref,
    left_ref,
    total_in,
    off_ref,
    act_ref,
    cnt_ref,
    cell_ref,
    offset_ref,
    job_ref,
    span_ref,
    new_ref,
    out_ref,
    tab_ref,
    near_ref,
    total_ref,
    names_a,
    names_b,
    made_ref,
    beta_ref,
    sems,
):
    cells = new_ref.shape[0]
    slots = act_ref.shape[0]
    me = own_index()
    odd = me % 2
    copies = start_copies(
        [
            (ref.at[pl.ds(PLANES * RIM, 8), :], names)
            for ref, names in ((a_ref, names_a), (b_ref, names_b))
        ],
        sems,
    )
    start_of_a = (1 - odd) * (cells + RIM)
    for in_ref, start in ((a_ref, start_of_a), (b_ref, cells + RIM - start_of_a)):
        put_table(tab_ref, start, RIM, *[in_ref[pl.ds(i * RIM, RIM), :] for i in range(PLANES)])

    jobs = job_ref[0]

    def late_entry(job, place, weight):
        tile = stencil_tile(tab_ref, off_ref, cell_ref[place], offset_ref[place])
        span = pl.ds(pl.multiple_of(span_ref[job], P_SIZE), P_SIZE)
        outer, inner, kept = density_terms(left_ref[span, :], [tile], [weight])
        total_ref[span, :] = total_ref[span, :] + (outer - 4.0 * inner)
        return kept[0]

    @pl.loop(JOBS, jobs)
    def _(job):
        place = job_ref[job + 1]
        near_ref[pl.ds(pl.multiple_of(place * 8, 8), 8), :] = late_entry(job, place, None)

    for turn in range(JOBS):
        valid = turn < jobs
        job = jnp.where(valid, turn, 0)
        place = jnp.where(valid, job_ref[turn + 1], 0)
        kept = late_entry(job, place, jnp.where(valid, 1.0, 0.0))
        target = jnp.where(valid, place, slots * NBR)
        near_ref[pl.ds(pl.multiple_of(target * 8, 8), 8), :] = kept

    for slot in range(slots):
        mine = act_ref[slot] - me * cells
        inverse_len = tile_of(tab_ref, RIM + mine)[6:7, :]
        span = pl.ds(slot * P_SIZE, P_SIZE)
        left = left_ref[span, :]
        outer_sum = jnp.zeros((P_SIZE, P_SIZE), f32)
        inner_sum = jnp.zeros((P_SIZE, P_SIZE), f32)
        for first in range(early(slot), NBR, 2):
            positions = range(first, min(first + 2, NBR))
            tiles = []
            for position in positions:
                place = place_of(slot, position)
                tiles.append(stencil_tile(tab_ref, off_ref, cell_ref[place], offset_ref[place]))
            outer, inner, kept = density_terms(left, tiles, [None] * len(tiles))
            outer_sum, inner_sum = outer_sum + outer, inner_sum + inner
            for position, tile in zip(positions, kept):
                near_ref[pl.ds(place_of(slot, position) * 8, 8), :] = tile
        total = total_ref[span, :] + (outer_sum - 4.0 * inner_sum)
        made = row_sums(total) * (2.0 * kernel_norm) * inverse_len * inverse_len * inverse_len
        made = jnp.where(slot < cnt_ref[0], made, new_ref[pl.ds(mine, 1), :])
        beta = beta_of(inverse_len, ent_ref[pl.ds(mine, 1), :], made)
        made_ref[slot : slot + 1, :] = made
        beta_ref[slot : slot + 1, :] = beta

    for slot in range(slots):
        mine = act_ref[slot] - me * cells
        new_ref[pl.ds(mine, 1), :] = made_ref[slot : slot + 1, :]
        tab_ref[pl.ds((RIM + mine) * 8 + 7, 1), :] = beta_ref[slot : slot + 1, :]
    code = code_ref[...]
    chosen = jnp.zeros_like(code)
    for slot in range(slots):
        chosen = jnp.where(code == float(slot + 1), made_ref[slot : slot + 1, :], chosen)
    late = place_ref[...] * jnp.sum(chosen, axis=1, keepdims=True)
    targets = base_ref.shape[0]
    aim = lax.broadcasted_iota(jnp.int32, (targets, P_SIZE), 0) == dest_ref[...]
    aim = jnp.where(aim, 1.0, 0.0)
    for line in range(1, 8):
        fill = jnp.zeros((1, P_SIZE), f32) if line > slots else beta_ref[line - 1 : line, :]
        put(out_ref, 0, targets, line, jnp.broadcast_to(fill, (targets, P_SIZE)))
    sent = base_ref[...] + jnp.dot(
        aim, late, precision=lax.Precision.HIGHEST, preferred_element_type=f32
    )
    put(out_ref, 0, targets, 0, sent)
    for copy in copies:
        copy.wait()


def spline(base, slope, distance):
    step = distance * slope
    outer = jnp.maximum(base - step, 0.0)
    least = jnp.minimum(step, outer)
    return least * (outer + (outer - least))


def pull_sums(pulls, nears):
    row = row_ids()
    highs = [pull.astype(bf16) for pull in pulls]
    lows = [(pull - high.astype(f32)).astype(bf16) for pull, high in zip(pulls, highs)]
    sides = []
    for near in nears:
        weighed = jnp.where(row < 3, near, 1.0) * near[5:6, :]
        sides.append(jnp.concatenate(split(weighed), axis=0).astype(bf16))
    return lax.dot_general(
        jnp.concatenate(highs + lows, axis=1),
        jnp.concatenate(sides + sides, axis=1),
        (((1,), (1,)), ((), ())),
        preferred_element_type=f32,
    )


def force_kernel(
    tab_ref,
    near_ref,
    new_ref,
    names_a,
    names_b,
    act_ref,
    cnt_ref,
    cell_ref,
    acc_out,
    list_ref,
    new_out,
    left_ref,
    sems,
):
    cells = tab_ref.shape[0] // 8 - 2 * RIM
    me = own_index()
    odd = me % 2
    slots = act_ref.shape[0]
    copies = start_copies([(new_ref, new_out)], sems)
    fa = [names_a[0, s].astype(jnp.int32) for s in range(slots)]
    fb = [names_b[0, s].astype(jnp.int32) for s in range(slots)]
    left = [jnp.where(odd == 1, fa[s], fb[s]) for s in range(slots)]
    right = [jnp.where(odd == 1, fb[s], fa[s]) for s in range(slots)]
    left = [jnp.where(v >= cells - RIM, v - (cells - RIM), -1) for v in left]
    right = [jnp.where(jnp.logical_and(v >= 0, v < RIM), v + cells + RIM, -1) for v in right]
    at = jnp.int32(0)
    for slot in range(slots):
        live = slot < cnt_ref[0]
        mine = act_ref[slot] - me * cells
        own = tile_of(tab_ref, RIM + mine)
        columns = own.T
        own_base = jnp.broadcast_to(columns[:, 7:8], (P_SIZE, P_SIZE))
        own_slope = own_base * jnp.broadcast_to(columns[:, 6:7], (P_SIZE, P_SIZE))
        left_side = own_features(own, 1.0)
        left_ref[pl.ds(slot * P_SIZE, P_SIZE), :] = left_side
        sums = jnp.zeros((P_SIZE, 24), f32)
        for block in groups(SUM_GROUP):
            pulls, nears = [], []
            for first in range(block.start, block.stop, 2):
                group = range(first, min(first + 2, block.stop))
                tiles = [near_ref[pl.ds((slot * NBR + entry) * 8, 8), :] for entry in group]
                other = jnp.concatenate([other_features(tile) for tile in tiles], axis=1)
                squares = jnp.dot(left_side, other, preferred_element_type=f32)
                for place, entry in enumerate(group):
                    near = tiles[place]
                    cell = cell_ref[place_of(slot, entry)]
                    found = jnp.int32(-1)
                    for s in range(slots):
                        found = jnp.where(cell == left[s], s, found)
                        found = jnp.where(cell == right[s], slots + s, found)
                    list_ref[at + 1] = (slot * NBR + entry) * (2 * slots) + found
                    at = at + jnp.where(jnp.logical_and(found >= 0, live), 1, 0)

                    beta = tab_ref[pl.ds(cell * 8 + 7, 1), :]
                    slope = beta * near[6:7, :]
                    square = jnp.maximum(squares[:, place * P_SIZE : (place + 1) * P_SIZE], near[6:7, :] * TINY)
                    inverse = lax.rsqrt(square)
                    distance = square * inverse
                    pull = spline(own_base, own_slope, distance) + spline(beta, slope, distance)
                    pull = pull * inverse
                    pulls.append(pull)
                    nears.append(near)
            sums = sums + pull_sums(pulls, nears)
        flat = sums.T
        flat = flat[0:8, :] + flat[8:16, :] + flat[16:24, :]
        made = jnp.where(live, own * flat[3:4, :] - flat, 0.0)
        for axis in range(3):
            acc_out[axis, slot : slot + 1, :] = made[axis : axis + 1, :]
    list_ref[0] = at
    for copy in copies:
        copy.wait()


def finish_kernel(
    capacity,
    tab_ref,
    near_ref,
    part_ref,
    got_ref,
    pick_ref,
    left_ref,
    list_ref,
    act_ref,
    acc_out,
    arrive_ref,
    late_ref,
):
    cells = tab_ref.shape[0] // 8 - 2 * RIM
    me = own_index()
    slots = act_ref.shape[0]
    targets = got_ref.shape[0] // 8
    acc_out[...] = part_ref[...]
    rows = got_ref[pl.ds(0, targets, stride=8), :]
    width = targets * capacity
    sender = lax.broadcasted_iota(jnp.int32, (targets, width), 1) // capacity
    mask = sender == lax.broadcasted_iota(jnp.int32, (targets, width), 0)
    pieces = jnp.concatenate(split(rows), axis=0).astype(bf16)
    spread = jnp.dot(pieces, pick_ref[...], preferred_element_type=f32)
    spread = spread[0:targets] + spread[targets : 2 * targets] + spread[2 * targets :]
    for index in range(STATE):
        part = spread[:, index * width : (index + 1) * width]
        arrive_ref[index : index + 1, :] = jnp.sum(jnp.where(mask, part, 0.0), axis=0, keepdims=True)

    count = list_ref[0]

    @pl.when(count > 0)
    def _():
        late_ref[...] = jnp.zeros_like(late_ref)

        @pl.loop(0, (count + ITEMS - 1) // ITEMS)
        def _(block):
            made = []
            for step in range(ITEMS):
                item = block * ITEMS + step
                word = list_ref[jnp.minimum(item, count - 1) + 1]
                found = word % (2 * slots)
                place = word // (2 * slots)
                slot = place // NBR
                span = pl.ds(pl.multiple_of(slot * P_SIZE, P_SIZE), P_SIZE)
                other = jnp.where(found < slots, me - 1, me + 1)
                near = near_ref[pl.ds(pl.multiple_of(place * 8, 8), 8), :]
                beta = got_ref[pl.ds(other * 8 + 1 + found % slots, 1), :]
                beta = beta * jnp.where(item < count, 1.0, 0.0)
                square = jnp.dot(
                    left_ref[span, :], other_features(near), preferred_element_type=f32
                )
                square = jnp.maximum(square, near[6:7, :] * TINY)
                inverse = lax.rsqrt(square)
                pull = spline(beta, beta * near[6:7, :], square * inverse) * inverse
                made.append((span, pull_sums([pull], [near])))
            for span, sums in made:
                late_ref[span, :] = late_ref[span, :] + sums

        for slot in range(slots):
            own = tile_of(tab_ref, RIM + act_ref[slot] - me * cells)
            flat = late_ref[pl.ds(slot * P_SIZE, P_SIZE), :].T
            flat = flat[0:8, :] + flat[8:16, :] + flat[16:24, :]
            made = own * flat[3:4, :] - flat
            for axis in range(3):
                acc_out[axis, slot : slot + 1, :] += made[axis : axis + 1, :]


def local(
    positions,
    masses,
    smoothing,
    entropy,
    density,
    active_cells,
    active_count,
    neighbours,
    mig_source,
    mig_dest,
):
    cells = masses.shape[0]
    slots = active_cells.shape[0]
    devices = lax.axis_size(AXES)
    mig_rows = mig_source.shape[0]
    capacity = max(2, 2 * mig_rows // devices)
    shape = jax.ShapeDtypeStruct
    rim_shape = shape((PLANES * RIM + 8, P_SIZE), f32)
    tab_shape = pltpu.VMEM(((cells + 2 * RIM) * 8, P_SIZE), f32)
    near_shape = pltpu.VMEM(((slots * NBR + 1) * 8, P_SIZE), f32)
    name_shape = pltpu.SMEM((8, P_SIZE), f32)
    fields = (positions, masses, smoothing, entropy, density)
    rows = (mig_source.reshape(1, mig_rows), mig_dest.reshape(1, mig_rows))
    lists = (active_cells, neighbours)

    raw = [in_hbm(v) for v in fields]
    send_b, send_a, active, near_ids = pl.pallas_call(
        pack_kernel,
        out_shape=(rim_shape, rim_shape) + tuple(pltpu.SMEM(v.shape, v.dtype) for v in lists),
        in_specs=[HBM] * 7 + [SMEM],
        out_specs=(VMEM,) * 2 + (SMEM,) * 2,
        scratch_shapes=[
            pltpu.VMEM((2, 3, RIM, P_SIZE), f32),
            pltpu.SemaphoreType.DMA((16,)),
        ],
        compiler_params=PARAMS,
        name="pack",
    )(*raw, *[in_hbm(v) for v in lists], active_count)

    pairs_a = [(i ^ 1, i) for i in range(devices) if i ^ 1 < devices]
    pairs_b = []
    for i in range(1, devices - 1, 2):
        pairs_b += [(i, i + 1), (i + 1, i)]
    got_b = lax.ppermute(send_b, AXES, pairs_b)
    got_a = lax.ppermute(send_a, AXES, pairs_a)

    ent, rho, dest, table, base, code, place, pick, near, left, total, offsets, *found = pl.pallas_call(
        functools.partial(migrant_kernel, capacity),
        out_shape=(
            pltpu.VMEM((cells, P_SIZE), f32),
            pltpu.VMEM((cells, P_SIZE), f32),
            pltpu.VMEM((1, mig_rows), jnp.int32),
            tab_shape,
            pltpu.VMEM((devices, P_SIZE), f32),
            pltpu.VMEM((mig_rows, P_SIZE), f32),
            pltpu.VMEM((mig_rows, P_SIZE), f32),
            pltpu.VMEM((P_SIZE, STATE * devices * capacity), bf16),
            near_shape,
            pltpu.VMEM((slots * P_SIZE, 48), bf16),
            pltpu.VMEM((slots * P_SIZE, P_SIZE), f32),
            pltpu.VMEM((NBR * 8, P_SIZE), f32),
            pltpu.SMEM((slots * NBR,), jnp.int32),
            pltpu.SMEM((slots * NBR,), jnp.int32),
            pltpu.SMEM((slots * NBR + 2,), jnp.int32),
            pltpu.SMEM((slots * NBR + 1,), jnp.int32),
        ),
        in_specs=[HBM] * 7 + [SMEM] * 3,
        out_specs=(VMEM,) * 12 + (SMEM,) * 4,
        scratch_shapes=[
            pltpu.VMEM((3, cells, P_SIZE), f32),
            pltpu.VMEM((cells, P_SIZE), f32),
            pltpu.VMEM((cells, P_SIZE), f32),
            pltpu.VMEM((1, mig_rows), jnp.int32),
            pltpu.SemaphoreType.DMA((7,)),
        ],
        compiler_params=PARAMS,
        name="migrants",
    )(*raw, *[in_hbm(v) for v in rows], active, active_count, near_ids)

    made, outgoing, table, near, _, names_a, names_b = pl.pallas_call(
        density_kernel,
        out_shape=(
            pltpu.VMEM((cells, P_SIZE), f32),
            shape((devices * 8, P_SIZE), f32),
            tab_shape,
            near_shape,
            pltpu.VMEM((slots * P_SIZE, P_SIZE), f32),
            name_shape,
            name_shape,
        ),
        in_specs=[VMEM] * 13 + [SMEM] * 6,
        out_specs=(VMEM,) * 5 + (SMEM,) * 2,
        input_output_aliases={0: 0, 4: 2, 5: 3, 11: 4},
        scratch_shapes=[
            pltpu.VMEM((8, P_SIZE), f32),
            pltpu.VMEM((8, P_SIZE), f32),
            pltpu.SemaphoreType.DMA((2,)),
        ],
        compiler_params=PARAMS,
        name="density",
    )(
        rho,
        ent,
        got_a,
        got_b,
        table,
        near,
        base,
        code,
        place,
        dest,
        left,
        total,
        offsets,
        active,
        active_count,
        *found,
    )

    incoming = lax.all_to_all(outgoing, AXES, split_axis=0, concat_axis=0, tiled=True)

    todo_len = pl.cdiv(slots * NBR + 2, P_SIZE) * P_SIZE
    partial, todo, new_density, left = pl.pallas_call(
        force_kernel,
        out_shape=(
            shape((3, slots, P_SIZE), f32),
            pltpu.SMEM((todo_len,), jnp.int32),
            shape((cells, P_SIZE), f32),
            pltpu.VMEM((slots * P_SIZE, 48), bf16),
        ),
        in_specs=[VMEM] * 3 + [SMEM] * 5,
        out_specs=(VMEM, SMEM, HBM, VMEM),
        scratch_shapes=[
            pltpu.SemaphoreType.DMA((1,)),
        ],
        compiler_params=PARAMS,
        name="force",
    )(table, near, made, names_a, names_b, active, active_count, found[0])

    acceleration, arrivals = pl.pallas_call(
        functools.partial(finish_kernel, capacity),
        out_shape=(
            shape((3, slots, P_SIZE), f32),
            shape((STATE, devices * capacity), f32),
        ),
        in_specs=[VMEM] * 6 + [SMEM] * 2,
        out_specs=(VMEM, VMEM),
        scratch_shapes=[pltpu.VMEM((slots * P_SIZE, 24), f32)],
        compiler_params=PARAMS,
        name="finish",
    )(table, near, partial, incoming, pick, left, todo, active)
    return (new_density, acceleration, arrivals)


def solution(mesh):
    placed = (
        P(None, AXES, None),
        P(AXES, None),
        P(AXES, None),
        P(AXES, None),
        P(AXES, None),
        P(AXES),
        P(AXES),
        P(AXES, None),
        P(AXES),
        P(AXES, None),
    )
    return jax.shard_map(
        local,
        mesh=mesh,
        in_specs=placed,
        out_specs=(P(AXES, None), P(None, AXES, None), P(None, AXES)),
        check_vma=False,
    )
```

profile of v0, /device:TPU:0, one launch (start us, length us, event | category | flops | bytes accessed | tf_op | source)
XLA Modules:
  0.0 31.7 jit_solution(8144056721486655272)
XLA Ops:
  1.3 1.1 %pack.1 = (f32[392,128]{1,0:T(8,128)S(1)}, f32[392,128]{1,0:T(8,128)S(1)}, s32[4]{0:T(128)S(4)}, s32[4,27]{1,0:T(4,128)S(4)}) custom-call(f32[3,256,128]{2,1,0:T(8,128)} %pos_hbm.3, f32[256,128]{1,0:T(8,128)} %mass_hbm.3, f32[256,128]{1,0:T(8,128)} %len_hbm.3, f32[256,128]{1,0:T(8,128)} %ent_hbm.3, f32[256,128]{1,0:T(8,128)} %rho_hbm.3, s32[4]{0:T(128)} %act_hbm.1, ...), custom_call_target="tpu_custom_call" | custom-call | tf_op jit(solution)/shard_map/pack/pallas_call | solution.py:665
  2.4 0.6 %collective-permute-start = (f32[392,128]{1,0:T(8,128)S(1)}, f32[392,128]{1,0:T(8,128)S(1)}, u32[]{:S(2)}, u32[]{:S(2)}) collective-permute-start(f32[392,128]{1,0:T(8,128)S(1)} %get-tuple-element.39), channel_id=1, source_target_pairs={{1,0},{0,1},{3,2},{2,3},{5,4},{4,5},{7,6},{6,7},{9,8},{8,9},{11,10... | collective-permute-start | bytes 602120 | tf_op jit(solution)/shard_map/ppermute | solution.py:683
  3.0 0.7 %collective-permute-start.1 = (f32[392,128]{1,0:T(8,128)S(1)}, f32[392,128]{1,0:T(8,128)S(1)}, u32[]{:S(2)}, u32[]{:S(2)}) collective-permute-start(f32[392,128]{1,0:T(8,128)S(1)} %get-tuple-element.40), channel_id=1, source_target_pairs={{1,2},{2,1},{3,4},{4,3},{5,6},{6,5},{7,8},{8,7},{9,10},{10,9},{11,... | collective-permute-start | bytes 602120 | tf_op jit(solution)/shard_map/ppermute | solution.py:682
  3.6 4.1 %migrants.1 = (f32[256,128]{1,0:T(8,128)S(1)}, f32[256,128]{1,0:T(8,128)S(1)}, s32[1,128]{1,0:T(1,128)S(1)}, f32[3072,128]{1,0:T(8,128)S(1)}, f32[32,128]{1,0:T(...) custom-call(f32[3,256,128]{2,1,0:T(8,128)} %pos_hbm.3, ...), custom_call_target="tpu_custom_call" | custom-call | tf_op jit(solution)/shard_map/migrants/pallas_call | solution.py:685
  7.8 0.0 collective-permute-done.a_ref
  7.8 0.0 collective-permute-done.1.b_ref
  7.8 3.9 %density.1 = (f32[256,128]{1,0:T(8,128)S(1)}, f32[256,128]{1,0:T(8,128)}, f32[3072,128]{1,0:T(8,128)S(1)}, f32[872,128]{1,0:T(8,128)S(1)}, f32[512,128]{1,0:T(8,...) custom-call(f32[256,128]{1,0:T(8,128)S(1)} %get-tuple-element.37.rho, ...), custom_call_target="tpu_custom_call", output_to_operand_aliasing={{0}: (0, {}), {2}: (4, {}), {3}: (5, {}), {4}: (11, {})} | custom-call | tf_op jit(solution)/shard_map/density/pallas_call | solution.py:718
  11.7 11.1 %all-to-all-start = ((f32[32,8,128]{2,1,0:T(8,128)}), f32[32,8,128]{2,1,0:T(8,128)S(1)}, u32[]{:S(2)}, u32[]{:S(2)}) async-start(f32[32,8,128]{2,1,0:T(8,128)} %bitcast.2), calls=%async_computation | async-start | bytes 262144 | tf_op jit(solution)/shard_map/all_to_all | solution.py:758
  22.8 7.5 %force.1 = (f32[3,4,128]{2,1,0:T(4,128)S(1)}, s32[128]{0:T(128)S(4)}, f32[256,128]{1,0:T(8,128)}, bf16[512,48]{1,0:T(8,128)(2,1)S(1)}) custom-call(f32[3072,128]{1,0:T(8,128)S(1)} %get-tuple-element.54.tab_ref, f32[872,128]{1,0:T(8,128)S(1)} %get-tuple-element.55.near_ref, f32[256,128]{1,0:T(8,128)S(1)} %get-tuple-element.56.new_ref, ...), custom_call_target="tpu_custom_call" | custom-call | tf_op jit(solution)/shard_map/force/pallas_call | solution.py:761
  30.3 0.5 %all-to-all-done = f32[32,8,128]{2,1,0:T(8,128)S(1)} async-done(((f32[32,8,128]{2,1,0:T(8,128)}), f32[32,8,128]{2,1,0:T(8,128)S(1)}, u32[]{:S(2)}, u32[]{:S(2)}) %all-to-all-start) | async-done | bytes 131104 | tf_op jit(solution)/shard_map/all_to_all | solution.py:758
  30.8 0.9 %finish.1 = (f32[3,4,128]{2,1,0:T(4,128)}, f32[7,256]{1,0:T(8,128)}) custom-call(f32[3072,128]{1,0:T(8,128)S(1)} %get-tuple-element.54.tab_ref, f32[872,128]{1,0:T(8,128)S(1)} %get-tuple-element.55.near_ref, f32[3,4,128]{2,1,0:T(4,128)S(1)} %get-tuple-element.60.part_ref, f32[256,128]{1,0:T(8,128)S(1)} %bitcast.4, ...), custom_call_target="tpu_custom_call" | custom-call | tf_op jit(solution)/shard_map/finish/pallas_call | solution.py:778
Async XLA Ops:
  2.4 5.4 %collective-permute-start = (f32[392,128]{1,0:T(8,128)S(1)}, f32[392,128]{1,0:T(8,128)S(1)}, u32[]{:S(2)}, u32[]{:S(2)}) collective-permute-start(f32[392,128]{1,0:T(8,128)S(1)} %get-tuple-element.39), channel_id=1, source_target_pairs={{1,0},{0,1},{3,2},{2,3},{5,4},{4,5},{7,6},{6,7},{9,8},{8,9},{11,10... | collective-permute-start | bytes 602120 | tf_op jit(solution)/shard_map/ppermute | solution.py:683
  3.0 4.8 %collective-permute-start.1 = (f32[392,128]{1,0:T(8,128)S(1)}, f32[392,128]{1,0:T(8,128)S(1)}, u32[]{:S(2)}, u32[]{:S(2)}) collective-permute-start(f32[392,128]{1,0:T(8,128)S(1)} %get-tuple-element.40), channel_id=1, source_target_pairs={{1,2},{2,1},{3,4},{4,3},{5,6},{6,5},{7,8},{8,7},{9,10},{10,9},{11,... | collective-permute-start | bytes 602120 | tf_op jit(solution)/shard_map/ppermute | solution.py:682
  11.7 19.1 %all-to-all-start = ((f32[32,8,128]{2,1,0:T(8,128)}), f32[32,8,128]{2,1,0:T(8,128)S(1)}, u32[]{:S(2)}, u32[]{:S(2)}) async-start(f32[32,8,128]{2,1,0:T(8,128)} %bitcast.2), calls=%async_computation | async-start | bytes 262144 | tf_op jit(solution)/shard_map/all_to_all | solution.py:758
where the time goes:
time: 32.2 us; the launch traced here: 31.7 us
  Pallas kernels  17.6 us (55%)
  starting transfers between devices  12.3 us (38%)
  between operations  1.34 us (4%)
  waiting for transfers between devices  0.49 us (2%)
    all_to_all x1, starting transfers between devices, local(): lax.all_to_all(outgoing, AXES, split_axis=0, concat_axis=0, tiled=True)  11.1 us
    pallas_call x1, Pallas kernels, local(): pl.pallas_call(force_kernel, out_shape=(shape((3, slots, P_SIZE), f32), p...  7.53 us
    pallas_call x1, Pallas kernels, local(): pl.pallas_call(functools.partial(migrant_kernel, capacity), out_shape=(pl...  4.13 us
    pallas_call x1, Pallas kernels, local(): pl.pallas_call(density_kernel, out_shape=(pltpu.VMEM((cells, P_SIZE), f32...  3.92 us
    pallas_call x1, Pallas kernels, local(): pl.pallas_call(pack_kernel, out_shape=(rim_shape, rim_shape) + tuple((plt...  1.14 us
    pallas_call x1, Pallas kernels, local(): pl.pallas_call(functools.partial(finish_kernel, capacity), out_shape=(sha...  0.86 us
    ppermute x1, starting transfers between devices, local(): got_b = lax.ppermute(send_b, AXES, pairs_b)  0.66 us
  transfers between devices with their start and end apart: 3, of which 1 were waited for; matrix products, arithmetic and copies ran while one was open for 0% of the time, Pallas kernels for 37%

commit v1 on v0

--- a/solution.py
+++ b/solution.py
@@ -96,7 +96,6 @@
     rho_hbm,
     act_hbm,
     nbr_hbm,
-    cnt_ref,
     b_ref,
     a_ref,
     act_ref,
@@ -130,15 +129,13 @@
     slots = act_ref.shape[0]
     for slot in range(slots):
         mine = act_ref[slot] - me * cells
-        live = slot < cnt_ref[0]
-        names = jnp.where(jnp.logical_and(lane == slot, live), mine.astype(f32), names)
+        names = jnp.where(lane == slot, mine.astype(f32), names)
     cell = lax.broadcasted_iota(jnp.int32, (RIM, P_SIZE), 0)
     for side, (out_ref, start) in enumerate(sides):
         inverse_len = 1.0 / rim_ref[side, 0]
         beta = beta_of(inverse_len, rim_ref[side, 1], rim_ref[side, 2])
         for slot in range(slots):
-            mine = jnp.where(slot < cnt_ref[0], act_ref[slot] - me * cells - start, -1)
-            beta = jnp.where(cell == mine, 0.0, beta)
+            beta = jnp.where(cell == act_ref[slot] - me * cells - start, 0.0, beta)
         out_ref[pl.ds(4 * RIM, RIM), :] = inverse_len
         out_ref[pl.ds(5 * RIM, RIM), :] = beta
         out_ref[pl.ds(PLANES * RIM, 8), :] = names
@@ -665,7 +662,7 @@
     send_b, send_a, active, near_ids = pl.pallas_call(
         pack_kernel,
         out_shape=(rim_shape, rim_shape) + tuple(pltpu.SMEM(v.shape, v.dtype) for v in lists),
-        in_specs=[HBM] * 7 + [SMEM],
+        in_specs=[HBM] * 7,
         out_specs=(VMEM,) * 2 + (SMEM,) * 2,
         scratch_shapes=[
             pltpu.VMEM((2, 3, RIM, P_SIZE), f32),
@@ -673,7 +670,8 @@
         ],
         compiler_params=PARAMS,
         name="pack",
-    )(*raw, *[in_hbm(v) for v in lists], active_count)
+    )(*raw, *[in_hbm(v) for v in lists])
+    send_b, active_count = lax.optimization_barrier((send_b, active_count))
 
     pairs_a = [(i ^ 1, i) for i in range(devices) if i ^ 1 < devices]
     pairs_b = []

time: 32.2 us -> 31.5 us (0.978)
  starting transfers between devices: 12.3 us -> 11.8 us
    all_to_all x1, starting transfers between devices: 11.1 us -> 6.77 us  [local(): lax.all_to_all(outgoing, AXES, split_axis=0, concat_axis=0, tiled=True)]
    ppermute x1, starting transfers between devices: 0.56 us -> 4.38 us  [local(): got_a = lax.ppermute(send_a, AXES, pairs_a)]
where the time goes in v1:
time: 31.5 us; the launch traced here: 31.2 us
  Pallas kernels  17.6 us (56%)
  starting transfers between devices  11.8 us (37%)
  between operations  1.35 us (4%)
  waiting for transfers between devices  0.48 us (2%)
    pallas_call x1, Pallas kernels, local(): pl.pallas_call(force_kernel, out_shape=(shape((3, slots, P_SIZE), f32), p...  7.54 us
    all_to_all x1, starting transfers between devices, local(): lax.all_to_all(outgoing, AXES, split_axis=0, concat_axis=0, tiled=True)  6.77 us
    ppermute x1, starting transfers between devices, local(): got_a = lax.ppermute(send_a, AXES, pairs_a)  4.38 us
    pallas_call x1, Pallas kernels, local(): pl.pallas_call(functools.partial(migrant_kernel, capacity), out_shape=(pl...  4.12 us
    pallas_call x1, Pallas kernels, local(): pl.pallas_call(density_kernel, out_shape=(pltpu.VMEM((cells, P_SIZE), f32...  3.92 us
    pallas_call x1, Pallas kernels, local(): pl.pallas_call(pack_kernel, out_shape=(rim_shape, rim_shape) + tuple((plt...  1.14 us
    pallas_call x1, Pallas kernels, local(): pl.pallas_call(functools.partial(finish_kernel, capacity), out_shape=(sha...  0.86 us
    ppermute x1, starting transfers between devices, local(): got_b = lax.ppermute(send_b, AXES, pairs_b)  0.67 us
  transfers between devices with their start and end apart: 3, of which 1 were waited for; matrix products, arithmetic and copies ran while one was open for 0% of the time, Pallas kernels for 37%

profile of v1, /device:TPU:0, one launch (start us, length us, event | category | flops | bytes accessed | tf_op | source)
XLA Modules:
  0.0 31.2 jit_solution(14411574383446798953)
XLA Ops:
  0.6 1.1 %pack.1 = (f32[392,128]{1,0:T(8,128)S(1)}, f32[392,128]{1,0:T(8,128)S(1)}, s32[4]{0:T(128)S(4)}, s32[4,27]{1,0:T(4,128)S(4)}) custom-call(f32[3,256,128]{2,1,0:T(8,128)} %pos_hbm.3, f32[256,128]{1,0:T(8,128)} %mass_hbm.3, f32[256,128]{1,0:T(8,128)} %len_hbm.3, f32[256,128]{1,0:T(8,128)} %ent_hbm.3, f32[256,128]{1,0:T(8,128)} %rho_hbm.3, s32[4]{0:T(128)} %act_hbm.1, ...), custom_call_target="tpu_custom_call" | custom-call | tf_op jit(solution)/shard_map/pack/pallas_call | solution.py:662
  1.8 0.7 %collective-permute-start.1 = (f32[392,128]{1,0:T(8,128)S(1)}, f32[392,128]{1,0:T(8,128)S(1)}, u32[]{:S(2)}, u32[]{:S(2)}) collective-permute-start(f32[392,128]{1,0:T(8,128)S(1)} %get-tuple-element.44), channel_id=1, source_target_pairs={{1,2},{2,1},{3,4},{4,3},{5,6},{6,5},{7,8},{8,7},{9,10},{10,9},{11,... | collective-permute-start | bytes 602120 | tf_op jit(solution)/shard_map/ppermute | solution.py:680
  2.5 4.4 %collective-permute-start = (f32[392,128]{1,0:T(8,128)S(1)}, f32[392,128]{1,0:T(8,128)S(1)}, u32[]{:S(2)}, u32[]{:S(2)}) collective-permute-start(f32[392,128]{1,0:T(8,128)S(1)} %get-tuple-element.43), channel_id=1, source_target_pairs={{1,0},{0,1},{3,2},{2,3},{5,4},{4,5},{7,6},{6,7},{9,8},{8,9},{11,10... | collective-permute-start | bytes 602120 | tf_op jit(solution)/shard_map/ppermute | solution.py:681
  7.5 4.1 %migrants.1 = (f32[256,128]{1,0:T(8,128)S(1)}, f32[256,128]{1,0:T(8,128)S(1)}, s32[1,128]{1,0:T(1,128)S(1)}, f32[3072,128]{1,0:T(8,128)S(1)}, f32[32,128]{1,0:T(...) custom-call(f32[3,256,128]{2,1,0:T(8,128)} %pos_hbm.3, ...), custom_call_target="tpu_custom_call" | custom-call | tf_op jit(solution)/shard_map/migrants/pallas_call | solution.py:683
  11.6 0.0 collective-permute-done.1.b_ref
  11.6 0.0 collective-permute-done.a_ref
  11.6 3.9 %density.1 = (f32[256,128]{1,0:T(8,128)S(1)}, f32[256,128]{1,0:T(8,128)}, f32[3072,128]{1,0:T(8,128)S(1)}, f32[872,128]{1,0:T(8,128)S(1)}, f32[512,128]{1,0:T(8,...) custom-call(f32[256,128]{1,0:T(8,128)S(1)} %get-tuple-element.41.rho, ...), custom_call_target="tpu_custom_call", output_to_operand_aliasing={{0}: (0, {}), {2}: (4, {}), {3}: (5, {}), {4}: (11, {})} | custom-call | tf_op jit(solution)/shard_map/density/pallas_call | solution.py:716
  15.6 6.8 %all-to-all-start = ((f32[32,8,128]{2,1,0:T(8,128)}), f32[32,8,128]{2,1,0:T(8,128)S(1)}, u32[]{:S(2)}, u32[]{:S(2)}) async-start(f32[32,8,128]{2,1,0:T(8,128)} %bitcast.2), calls=%async_computation | async-start | bytes 262144 | tf_op jit(solution)/shard_map/all_to_all | solution.py:756
  22.4 7.5 %force.1 = (f32[3,4,128]{2,1,0:T(4,128)S(1)}, s32[128]{0:T(128)S(4)}, f32[256,128]{1,0:T(8,128)}, bf16[512,48]{1,0:T(8,128)(2,1)S(1)}) custom-call(f32[3072,128]{1,0:T(8,128)S(1)} %get-tuple-element.58.tab_ref, f32[872,128]{1,0:T(8,128)S(1)} %get-tuple-element.59.near_ref, f32[256,128]{1,0:T(8,128)S(1)} %get-tuple-element.60.new_ref, ...), custom_call_target="tpu_custom_call" | custom-call | tf_op jit(solution)/shard_map/force/pallas_call | solution.py:759
  29.9 0.5 %all-to-all-done = f32[32,8,128]{2,1,0:T(8,128)S(1)} async-done(((f32[32,8,128]{2,1,0:T(8,128)}), f32[32,8,128]{2,1,0:T(8,128)S(1)}, u32[]{:S(2)}, u32[]{:S(2)}) %all-to-all-start) | async-done | bytes 131104 | tf_op jit(solution)/shard_map/all_to_all | solution.py:756
  30.4 0.9 %finish.1 = (f32[3,4,128]{2,1,0:T(4,128)}, f32[7,256]{1,0:T(8,128)}) custom-call(f32[3072,128]{1,0:T(8,128)S(1)} %get-tuple-element.58.tab_ref, f32[872,128]{1,0:T(8,128)S(1)} %get-tuple-element.59.near_ref, f32[3,4,128]{2,1,0:T(4,128)S(1)} %get-tuple-element.64.part_ref, f32[256,128]{1,0:T(8,128)S(1)} %bitcast.4, ...), custom_call_target="tpu_custom_call" | custom-call | tf_op jit(solution)/shard_map/finish/pallas_call | solution.py:776
Async XLA Ops:
  1.8 9.9 %collective-permute-start.1 = (f32[392,128]{1,0:T(8,128)S(1)}, f32[392,128]{1,0:T(8,128)S(1)}, u32[]{:S(2)}, u32[]{:S(2)}) collective-permute-start(f32[392,128]{1,0:T(8,128)S(1)} %get-tuple-element.44), channel_id=1, source_target_pairs={{1,2},{2,1},{3,4},{4,3},{5,6},{6,5},{7,8},{8,7},{9,10},{10,9},{11,... | collective-permute-start | bytes 602120 | tf_op jit(solution)/shard_map/ppermute | solution.py:680
  2.5 9.2 %collective-permute-start = (f32[392,128]{1,0:T(8,128)S(1)}, f32[392,128]{1,0:T(8,128)S(1)}, u32[]{:S(2)}, u32[]{:S(2)}) collective-permute-start(f32[392,128]{1,0:T(8,128)S(1)} %get-tuple-element.43), channel_id=1, source_target_pairs={{1,0},{0,1},{3,2},{2,3},{5,4},{4,5},{7,6},{6,7},{9,8},{8,9},{11,10... | collective-permute-start | bytes 602120 | tf_op jit(solution)/shard_map/ppermute | solution.py:681
  15.6 14.8 %all-to-all-start = ((f32[32,8,128]{2,1,0:T(8,128)}), f32[32,8,128]{2,1,0:T(8,128)S(1)}, u32[]{:S(2)}, u32[]{:S(2)}) async-start(f32[32,8,128]{2,1,0:T(8,128)} %bitcast.2), calls=%async_computation | async-start | bytes 262144 | tf_op jit(solution)/shard_map/all_to_all | solution.py:756

commit v2 on v1

--- a/solution.py
+++ b/solution.py
@@ -455,13 +455,12 @@
     targets = base_ref.shape[0]
     aim = lax.broadcasted_iota(jnp.int32, (targets, P_SIZE), 0) == dest_ref[...]
     aim = jnp.where(aim, 1.0, 0.0)
-    for line in range(1, 8):
-        fill = jnp.zeros((1, P_SIZE), f32) if line > slots else beta_ref[line - 1 : line, :]
-        put(out_ref, 0, targets, line, jnp.broadcast_to(fill, (targets, P_SIZE)))
+    for slot in range(slots):
+        out_ref[:, 1 + slot, 0, :] = jnp.broadcast_to(beta_ref[slot : slot + 1, :], (targets, P_SIZE))
     sent = base_ref[...] + jnp.dot(
         aim, late, precision=lax.Precision.HIGHEST, preferred_element_type=f32
     )
-    put(out_ref, 0, targets, 0, sent)
+    out_ref[:, 0, 0, :] = sent
     for copy in copies:
         copy.wait()
 
@@ -580,9 +579,9 @@
     cells = tab_ref.shape[0] // 8 - 2 * RIM
     me = own_index()
     slots = act_ref.shape[0]
-    targets = got_ref.shape[0] // 8
+    targets = got_ref.shape[0]
     acc_out[...] = part_ref[...]
-    rows = got_ref[pl.ds(0, targets, stride=8), :]
+    rows = got_ref[:, 0, 0, :]
     width = targets * capacity
     sender = lax.broadcasted_iota(jnp.int32, (targets, width), 1) // capacity
     mask = sender == lax.broadcasted_iota(jnp.int32, (targets, width), 0)
@@ -611,7 +610,7 @@
                 span = pl.ds(pl.multiple_of(slot * P_SIZE, P_SIZE), P_SIZE)
                 other = jnp.where(found < slots, me - 1, me + 1)
                 near = near_ref[pl.ds(pl.multiple_of(place * 8, 8), 8), :]
-                beta = got_ref[pl.ds(other * 8 + 1 + found % slots, 1), :]
+                beta = got_ref[other, 1 + found % slots]
                 beta = beta * jnp.where(item < count, 1.0, 0.0)
                 square = jnp.dot(
                     left_ref[span, :], other_features(near), preferred_element_type=f32
@@ -717,7 +716,7 @@
         density_kernel,
         out_shape=(
             pltpu.VMEM((cells, P_SIZE), f32),
-            shape((devices * 8, P_SIZE), f32),
+            shape((devices, 1 + slots, 1, P_SIZE), f32),
             tab_shape,
             near_shape,
             pltpu.VMEM((slots * P_SIZE, P_SIZE), f32),

time: 31.5 us -> 31.2 us (level)
  waiting for transfers between devices: 0.48 us -> 0.01 us
    all_to_all x1, waiting for transfers between devices: 0.48 us -> 0.01 us  [local(): lax.all_to_all(outgoing, AXES, split_axis=0, concat_axis=0, tiled=True)]
  transfers between devices with their start and end apart: 3 -> 3, of which waited for: 1 -> 0; matrix products, arithmetic and copies ran while one was open for 0% -> 0% of each run, Pallas kernels for 37% -> 38%
where the time goes in v2:
time: 31.2 us; the launch traced here: 30.8 us
  Pallas kernels  17.6 us (56%)
  starting transfers between devices  11.8 us (38%)
  between operations  1.35 us (4%)
    pallas_call x1, Pallas kernels, local(): pl.pallas_call(force_kernel, out_shape=(shape((3, slots, P_SIZE), f32), p...  7.54 us
    all_to_all x1, starting transfers between devices, local(): lax.all_to_all(outgoing, AXES, split_axis=0, concat_axis=0, tiled=True)  6.78 us
    ppermute x1, starting transfers between devices, local(): got_a = lax.ppermute(send_a, AXES, pairs_a)  4.38 us
    pallas_call x1, Pallas kernels, local(): pl.pallas_call(functools.partial(migrant_kernel, capacity), out_shape=(pl...  4.12 us
    pallas_call x1, Pallas kernels, local(): pl.pallas_call(density_kernel, out_shape=(pltpu.VMEM((cells, P_SIZE), f32...  3.9 us
    pallas_call x1, Pallas kernels, local(): pl.pallas_call(pack_kernel, out_shape=(rim_shape, rim_shape) + tuple((plt...  1.14 us
    pallas_call x1, Pallas kernels, local(): pl.pallas_call(functools.partial(finish_kernel, capacity), out_shape=(sha...  0.88 us
    ppermute x1, starting transfers between devices, local(): got_b = lax.ppermute(send_b, AXES, pairs_b)  0.67 us
  transfers between devices with their start and end apart: 3, of which 0 were waited for; matrix products, arithmetic and copies ran while one was open for 0% of the time, Pallas kernels for 38%

profile of v2, /device:TPU:0, one launch (start us, length us, event | category | flops | bytes accessed | tf_op | source)
XLA Modules:
  0.0 30.8 jit_solution(10696224478518967935)
XLA Ops:
  0.6 1.1 %pack.1 = (f32[392,128]{1,0:T(8,128)S(1)}, f32[392,128]{1,0:T(8,128)S(1)}, s32[4]{0:T(128)S(4)}, s32[4,27]{1,0:T(4,128)S(4)}) custom-call(f32[3,256,128]{2,1,0:T(8,128)} %pos_hbm.3, f32[256,128]{1,0:T(8,128)} %mass_hbm.3, f32[256,128]{1,0:T(8,128)} %len_hbm.3, f32[256,128]{1,0:T(8,128)} %ent_hbm.3, f32[256,128]{1,0:T(8,128)} %rho_hbm.3, s32[4]{0:T(128)} %act_hbm.1, ...), custom_call_target="tpu_custom_call" | custom-call | tf_op jit(solution)/shard_map/pack/pallas_call | solution.py:661
  1.8 0.7 %collective-permute-start.1 = (f32[392,128]{1,0:T(8,128)S(1)}, f32[392,128]{1,0:T(8,128)S(1)}, u32[]{:S(2)}, u32[]{:S(2)}) collective-permute-start(f32[392,128]{1,0:T(8,128)S(1)} %get-tuple-element.44), channel_id=1, source_target_pairs={{1,2},{2,1},{3,4},{4,3},{5,6},{6,5},{7,8},{8,7},{9,10},{10,9},{11,... | collective-permute-start | bytes 602120 | tf_op jit(solution)/shard_map/ppermute | solution.py:679
  2.5 4.4 %collective-permute-start = (f32[392,128]{1,0:T(8,128)S(1)}, f32[392,128]{1,0:T(8,128)S(1)}, u32[]{:S(2)}, u32[]{:S(2)}) collective-permute-start(f32[392,128]{1,0:T(8,128)S(1)} %get-tuple-element.43), channel_id=1, source_target_pairs={{1,0},{0,1},{3,2},{2,3},{5,4},{4,5},{7,6},{6,7},{9,8},{8,9},{11,10... | collective-permute-start | bytes 602120 | tf_op jit(solution)/shard_map/ppermute | solution.py:680
  7.5 4.1 %migrants.1 = (f32[256,128]{1,0:T(8,128)S(1)}, f32[256,128]{1,0:T(8,128)S(1)}, s32[1,128]{1,0:T(1,128)S(1)}, f32[3072,128]{1,0:T(8,128)S(1)}, f32[32,128]{1,0:T(...) custom-call(f32[3,256,128]{2,1,0:T(8,128)} %pos_hbm.3, ...), custom_call_target="tpu_custom_call" | custom-call | tf_op jit(solution)/shard_map/migrants/pallas_call | solution.py:682
  11.6 0.0 collective-permute-done.1.b_ref
  11.6 0.0 collective-permute-done.a_ref
  11.6 3.9 %density.1 = (f32[256,128]{1,0:T(8,128)S(1)}, f32[32,5,1,128]{3,2,1,0:T(1,128)}, f32[3072,128]{1,0:T(8,128)S(1)}, f32[872,128]{1,0:T(8,128)S(1)}, f32[512,128]{1...) custom-call(f32[256,128]{1,0:T(8,128)S(1)} %get-tuple-element.41.rho, ...), custom_call_target="tpu_custom_call", output_to_operand_aliasing={{0}: (0, {}), {2}: (4, {}), {3}: (5, {}), {4}: (11, {})} | custom-call | tf_op jit(solution)/shard_map/density/pallas_call | solution.py:715
  15.5 6.8 %all-to-all-start = ((f32[32,5,1,128]{3,2,1,0:T(1,128)}), f32[32,5,1,128]{3,2,1,0:T(1,128)S(1)}, u32[]{:S(2)}, u32[]{:S(2)}) async-start(f32[32,5,1,128]{3,2,1,0:T(1,128)} %get-tuple-element.65), calls=%async_computation | async-start | bytes 163840 | tf_op jit(solution)/shard_map/all_to_all | solution.py:755
  22.3 7.5 %force.1 = (f32[3,4,128]{2,1,0:T(4,128)S(1)}, s32[128]{0:T(128)S(4)}, f32[256,128]{1,0:T(8,128)}, bf16[512,48]{1,0:T(8,128)(2,1)S(1)}) custom-call(f32[3072,128]{1,0:T(8,128)S(1)} %get-tuple-element.58.tab_ref, f32[872,128]{1,0:T(8,128)S(1)} %get-tuple-element.59.near_ref, f32[256,128]{1,0:T(8,128)S(1)} %get-tuple-element.60.new_ref, ...), custom_call_target="tpu_custom_call" | custom-call | tf_op jit(solution)/shard_map/force/pallas_call | solution.py:758
  29.9 0.0 all-to-all-done.got_ref
  29.9 0.9 %finish.1 = (f32[3,4,128]{2,1,0:T(4,128)}, f32[7,256]{1,0:T(8,128)}) custom-call(f32[3072,128]{1,0:T(8,128)S(1)} %get-tuple-element.58.tab_ref, f32[872,128]{1,0:T(8,128)S(1)} %get-tuple-element.59.near_ref, f32[3,4,128]{2,1,0:T(4,128)S(1)} %get-tuple-element.64.part_ref, f32[32,5,1,128]{3,2,1,0:T(1,128)S(1)} %all-to-all-done.got_ref, ...), custom_call_target="tpu_custom_call" | custom-call | tf_op jit(solution)/shard_map/finish/pallas_call | solution.py:775
Async XLA Ops:
  1.8 9.8 %collective-permute-start.1 = (f32[392,128]{1,0:T(8,128)S(1)}, f32[392,128]{1,0:T(8,128)S(1)}, u32[]{:S(2)}, u32[]{:S(2)}) collective-permute-start(f32[392,128]{1,0:T(8,128)S(1)} %get-tuple-element.44), channel_id=1, source_target_pairs={{1,2},{2,1},{3,4},{4,3},{5,6},{6,5},{7,8},{8,7},{9,10},{10,9},{11,... | collective-permute-start | bytes 602120 | tf_op jit(solution)/shard_map/ppermute | solution.py:679
  2.5 9.2 %collective-permute-start = (f32[392,128]{1,0:T(8,128)S(1)}, f32[392,128]{1,0:T(8,128)S(1)}, u32[]{:S(2)}, u32[]{:S(2)}) collective-permute-start(f32[392,128]{1,0:T(8,128)S(1)} %get-tuple-element.43), channel_id=1, source_target_pairs={{1,0},{0,1},{3,2},{2,3},{5,4},{4,5},{7,6},{6,7},{9,8},{8,9},{11,10... | collective-permute-start | bytes 602120 | tf_op jit(solution)/shard_map/ppermute | solution.py:680
  15.5 14.3 %all-to-all-start = ((f32[32,5,1,128]{3,2,1,0:T(1,128)}), f32[32,5,1,128]{3,2,1,0:T(1,128)S(1)}, u32[]{:S(2)}, u32[]{:S(2)}) async-start(f32[32,5,1,128]{3,2,1,0:T(1,128)} %get-tuple-element.65), calls=%async_computation | async-start | bytes 163840 | tf_op jit(solution)/shard_map/all_to_all | solution.py:755
